TPU v7x, 32 devices: a whole 2x2x4 slice. The times are simulated.
32 devices in a mesh: ctx: 8 (over y, x, core), tp: 4 (over z).
Axes of the slice: x: 2, y: 2, z: 4, core: 2. Of those that a mesh axis runs over, the one named last changes fastest.
Arguments:
- query_rows: bfloat16 [8192, 4096], P('ctx', 'tp'), may hold values from -6 to 6
- key_rows: bfloat16 [8192, 4096], P('ctx', 'tp'), may hold values from -6 to 6
- value_rows: bfloat16 [8192, 4096], P('ctx', 'tp'), may hold values from -6 to 6
- layer_grad: bfloat16 [8192, 4096], P('ctx', 'tp'), may hold values from -6 to 6
- out_weight: bfloat16 [4096, 4096], P('tp'), may hold values from -0.09375 to 0.09375
Outputs:
- query_grad: bfloat16 [8192, 4096], P('ctx', 'tp')
- key_grad: bfloat16 [8192, 4096], P('ctx', 'tp')
- value_grad: bfloat16 [8192, 4096], P('ctx', 'tp')
All inputs are finite; a program needn't handle non-finite values.
Results may differ from a plain program's by a relative error of at most 0.0058.
Values may be sent and summed in bfloat16 or wider, within the bound.
A program may use at most 128 MiB of HBM per device.

v0:
```python
import jax
import jax.numpy as jnp
from jax import lax
from jax.sharding import PartitionSpec as P

HEAD = 128


def local(query_rows, key_rows, value_rows, layer_grad, out_weight):
    tokens = query_rows.shape[0]
    columns = query_rows.shape[1]
    head_count = columns // HEAD
    devices = lax.axis_size("ctx")
    myself = lax.axis_index("ctx")
    factor = float((HEAD * tokens * devices) ** (-0.5))
    grad_heads = lax.dot_general(
        lax.all_gather(layer_grad, "tp", axis=1, tiled=True),
        out_weight,
        (((1,), (1,)), ((), ())),
        preferred_element_type=jnp.float32,
    ).astype(jnp.bfloat16)
    query_three = query_rows.reshape(tokens, head_count, HEAD)
    key_three = key_rows.reshape(tokens, head_count, HEAD)
    value_three = value_rows.reshape(tokens, head_count, HEAD)
    gradient_three = grad_heads.reshape(tokens, head_count, HEAD)
    key_value_here = jnp.einsum(
        "lbg,lbz->bgz", key_three, value_three, preferred_element_type=jnp.float32
    )
    gradient_here = jnp.einsum(
        "lbg,lbz->bgz", query_three, gradient_three, preferred_element_type=jnp.float32
    )

    def pick_sum(stacked, lower):
        indices = jnp.arange(stacked.shape[0])
        chosen = indices < myself if lower else indices > myself
        return jnp.sum(jnp.where(chosen[:, None, None, None], stacked, jnp.float32(0.0)), 0)

    kv_before = pick_sum(lax.all_gather(key_value_here[None], "ctx", axis=0, tiled=True), True)
    grad_after = pick_sum(lax.all_gather(gradient_here[None], "ctx", axis=0, tiled=True), False)
    key_value_state = kv_before.astype(jnp.bfloat16)
    gradient_state = grad_after.astype(jnp.bfloat16)
    block_len = min(512, tokens)
    key_cols = jnp.arange(tokens)
    key_total = jnp.einsum(
        "yqr,qmr->yqm", value_three, gradient_state, preferred_element_type=jnp.float32
    )
    value_total = jnp.einsum(
        "jaq,aqd->jad", key_three, gradient_state, preferred_element_type=jnp.float32
    )
    query_parts = []
    for begin_row in range(0, tokens, block_len):
        query_blk = query_three[begin_row : begin_row + block_len]
        gradient_block = gradient_three[begin_row : begin_row + block_len]
        row_pos = begin_row + jnp.arange(block_len)
        causal = (row_pos[:, None] >= key_cols[None, :])[None]
        inside_gradient = jnp.einsum(
            "thv,shv->hts", gradient_block, value_three, preferred_element_type=jnp.float32
        )
        inside_gradient = jnp.where(causal, inside_gradient, jnp.float32(0.0)).astype(jnp.bfloat16)
        inside_query = jnp.einsum(
            "thk,shk->hts", query_blk, key_three, preferred_element_type=jnp.float32
        )
        inside_query = jnp.where(causal, inside_query, jnp.float32(0.0)).astype(jnp.bfloat16)
        query_part = jnp.einsum(
            "vmr,rve->mve", inside_gradient, key_three, preferred_element_type=jnp.float32
        )
        query_part = query_part + jnp.einsum(
            "nde,dze->ndz", gradient_block, key_value_state, preferred_element_type=jnp.float32
        )
        query_parts.append((factor * query_part).astype(jnp.bfloat16))
        key_total = key_total + jnp.einsum(
            "cxd,xcr->dcr", inside_gradient, query_blk, preferred_element_type=jnp.float32
        )
        value_total = value_total + jnp.einsum(
            "kzx,zkm->xkm", inside_query, gradient_block, preferred_element_type=jnp.float32
        )
    query_grad = jnp.concatenate(query_parts, 0).reshape(tokens, columns)
    key_grad = (factor * key_total).astype(jnp.bfloat16).reshape(tokens, columns)
    value_grad = (factor * value_total).astype(jnp.bfloat16).reshape(tokens, columns)
    return (query_grad, key_grad, value_grad)


def solution(mesh):
    return jax.shard_map(
        local,
        mesh=mesh,
        in_specs=(P("ctx", "tp"), P("ctx", "tp"), P("ctx", "tp"), P("ctx", "tp"), P("tp", None)),
        out_specs=(P("ctx", "tp"), P("ctx", "tp"), P("ctx", "tp")),
        check_vma=False,
    )
```

profile of v0, /device:TPU:0, one launch (start us, length us, event | category | flops | bytes accessed | tf_op | source)
XLA Modules:
  0.0 289.1 jit_solution(12135899003362094810)
XLA Ops:
  8.0 0.8 copy-done
  8.8 3.5 %fusion.7 = f32[8,128,128]{2,1,0:T(8,128)} fusion(bf16[1024,1024]{1,0:T(8,128)(2,1)S(1)} %copy-done, bf16[1024,1024]{1,0:T(8,128)(2,1)} %param.6), kind=kOutput, calls=%fused_computation.16 | convolution fusion | flops 268435456 | bytes 4718592 | tf_op jit(solution)/shard_map/lbg,lbz->bgz/dot_general | solution.py:26
  12.3 149.6 %all-gather.6.cloned.1.call-done = bf16[1024,4096]{1,0:T(8,128)(2,1)} async-done(((bf16[1024,1024]{1,0:T(8,128)(2,1)}), bf16[1024,4096]{1,0:T(8,128)(2,1)}) %all-gather.6.cloned.1.call-update) | async-done | bytes 8388624 | tf_op jit(solution)/shard_map/all_gather | solution.py:17
  161.9 13.9 %convolution_convert_fusion = bf16[1024,1024]{0,1:T(8,128)(2,1)S(1)} fusion(bf16[1024,4096]{1,0:T(8,128)(2,1)} %all-gather.6.cloned.1.call-done, bf16[1024,4096]{1,0:T(8,128)(2,1)} %param.9), kind=kOutput, calls=%fused_computation.39 | convolution fusion | flops 8590983168 | bytes 18874368 | tf_op jit(solution)/shard_map/dot_general | solution.py:16
  175.8 1.3 copy-done.7
  177.1 0.8 fusion.35
  177.9 1.0 copy.66
  178.9 2.7 fusion.54
  181.6 1.4 copy.68
  183.0 1.7 copy.69
  184.7 1.0 iota_compare_fusion.1
  185.7 1.2 iota_compare_fusion
  186.8 12.4 %all-gather.8.cloned.1.call-done = f32[64,128,128]{2,1,0:T(8,128)} async-done(((f32[8,128,128]{2,1,0:T(8,128)}), f32[64,128,128]{2,1,0:T(8,128)}) %all-gather.8.cloned.1.call-update) | async-done | bytes 4194320 | tf_op jit(solution)/shard_map/all_gather | solution.py:38
  199.2 2.9 select_reduce_fusion.1
  202.8 1.8 fusion.57
  204.6 5.9 %select_convert_fusion.3 = bf16[8,512,1024]{2,1,0:T(8,128)(2,1)} fusion(bf16[512,8,128]{0,2,1:T(8,128)(2,1)S(1)} %bitcast.147, pred[512,1024]{1,0:T(8,128)(4,1)S(1)} %copy-done.11, bf16[1024,1024]{1,0:T(8,128)(2,1)S(1)} %copy-done), kind=kOutput, calls=%fused_computation.3 | convolution fusion | flops 1082130432 | bytes 12058624 | tf_op jit(solution)/shard_map/thv,shv->hts/dot_general | solution.py:56
  210.5 2.6 select_convert_fusion.2
  213.2 8.9 %fusion.26 = bf16[512,8,128]{2,0,1:T(8,128)(2,1)S(1)} fusion(f32[8,128,512]{1,2,0:T(8,128)S(1)} %fusion.58, bf16[8,512,1024]{2,1,0:T(8,128)(2,1)} %select_convert_fusion.3, bf16[1024,1024]{1,0:T(8,128)(2,1)S(1)} %copy-done.5), kind=kOutput, calls=%fused_computation.36 | convolution fusion | flops 1075314688 | bytes 13631488 | tf_op jit(solution)/shard_map/vmr,rve->mve/dot_general | solution.py:64
  222.1 2.6 fusion.24
  224.7 1.5 pad_maximum_fusion
  226.2 3.9 %copy.64 = bf16[1024,8,128]{0,2,1:T(8,128)(2,1)} copy(bf16[1024,8,128]{2,0,1:T(8,128)(2,1)} %pad_maximum_fusion) | data formatting | bytes 4194304 | tf_op jit(solution)/shard_map/concatenate | solution.py:77
  230.1 3.9 %copy.76 = bf16[1024,1024]{1,0:T(8,128)(2,1)} copy(bf16[1024,1024]{0,1:T(8,128)(2,1)} %bitcast.136) | data formatting | bytes 4194304
  234.0 7.0 %fusion.56 = f32[8,1024,128]{1,2,0:T(8,128)} fusion(bf16[512,8,128]{0,2,1:T(8,128)(2,1)} %bitcast.139, bf16[8,512,1024]{2,1,0:T(8,128)(2,1)} %select_convert_fusion.3), kind=kOutput, calls=%fused_computation.64 | convolution fusion | flops 1073741824 | bytes 13631488 | tf_op jit(solution)/shard_map/cxd,xcr->dcr/dot_general | solution.py:71
  241.1 8.0 %fusion.2 = f32[8,128,1024]{2,1,0:T(8,128)} fusion(bf16[512,8,128]{0,2,1:T(8,128)(2,1)} %bitcast.148, bf16[512,8,128]{0,2,1:T(8,128)(2,1)} %bitcast.140, pred[512,1024]{1,0:T(8,128)(4,1)} %iota_compare_fusion.1, bf16[1024,1024]{1,0:T(8,128)(2,1)} %param.6), kind=kOutput, calls=%fused_computation.11 | convolution fusion | flops 2155872256 | bytes 8912896 | tf_op jit(solution)/shard_map/kzx,zkm->xkm/dot_general | solution.py:74
  249.1 7.7 %fusion.3 = f32[8,128,1024]{2,1,0:T(8,128)} fusion(bf16[512,8,128]{0,2,1:T(8,128)(2,1)} %bitcast.145, bf16[512,8,128]{0,2,1:T(8,128)(2,1)S(1)} %bitcast.137, pred[512,1024]{1,0:T(8,128)(4,1)} %iota_compare_fusion, bf16[1024,1024]{1,0:T(8,128)(2,1)} %param.6), kind=kOutput, calls=%fused_computation.12 | convolution fusion | flops 2155872256 | bytes 8912896 | tf_op jit(solution)/shard_map/kzx,zkm->xkm/dot_general | solution.py:74
  256.8 2.7 select_reduce_fusion
  259.5 0.7 fusion.18
  260.3 1.4 copy-done.1
  261.7 6.6 %fusion.1 = bf16[1024,8,128]{0,2,1:T(8,128)(2,1)} fusion(f32[8,1024,128]{1,2,0:T(8,128)S(1)} %copy-done.1, f32[8,128,1024]{2,1,0:T(8,128)S(1)} %fusion.18, bf16[512,8,128]{0,2,1:T(8,128)(2,1)S(1)} %bitcast.138, bf16[8,512,1024]{2,1,0:T(8,128)(2,1)} %copy-done.2), kind=kOutput, calls=%fused_computation.6 | convolution fusion | flops 1077936128 | bytes 19922944 | tf_op jit(solution)/shard_map/cxd,xcr->dcr/dot_general | solution.py:71
  268.3 3.9 %copy.77 = bf16[1024,1024]{1,0:T(8,128)(2,1)} copy(bf16[1024,1024]{0,1:T(8,128)(2,1)} %bitcast.134) | data formatting | bytes 4194304
  272.2 6.4 %multiply_convert_fusion = bf16[8,128,1024]{2,1,0:T(8,128)(2,1)} fusion(f32[8,128,1024]{2,1,0:T(8,128)} %fusion.3, f32[8,128,1024]{2,1,0:T(8,128)} %fusion.2, bf16[8,128,128]{2,1,0:T(8,128)(2,1)S(1)} %select_reduce_fusion, bf16[1024,1024]{1,0:T(8,128)(2,1)} %param.6), kind=kOutput, calls=%fused_computation.8 | convolution fusion | flops 272629760 | bytes 12845056 | tf_op jit(solution)/shard_map/jaq,aqd->jad/dot_general | solution.py:47
  278.6 3.9 %copy.78 = bf16[1024,1024]{1,0:T(8,128)(2,1)} copy(bf16[1024,1024]{0,1:T(8,128)(2,1)} %bitcast.135) | data formatting | bytes 4194304
  (33 shorter events, 1.6 us)
Async XLA Ops:
  7.2 1.6 copy-start
  7.2 154.7 %all-gather.6.cloned.1.call-start = ((), (), s32[]{:S(2)}) async-start(), calls=%async_computation | async-start | bytes 10485760 | tf_op jit(solution)/shard_map/all_gather | solution.py:17
  7.9 191.3 %all-gather.8.cloned.1.call-start = ((), (), s32[]{:S(2)}) async-start(), calls=%async_computation.1 | async-start | bytes 4718592 | tf_op jit(solution)/shard_map/all_gather | solution.py:38
  12.2 244.6 %all-gather.10.cloned.1.call-start = ((), (), s32[]{:S(2)}) async-start(), calls=%async_computation.2 | async-start | bytes 4718592 | tf_op jit(solution)/shard_map/all_gather | solution.py:39
  161.9 15.2 %copy-start.6 = (bf16[1024,1024]{1,0:T(8,128)(2,1)S(1)}, bf16[1024,1024]{1,0:T(8,128)(2,1)}, u32[]{:S(2)}) copy-start(bf16[1024,1024]{1,0:T(8,128)(2,1)} %param.5) | copy-start | bytes 6291460
  175.8 1.3 copy-start.7
  199.2 2.9 copy-start.8
  202.2 2.4 copy-start.4
  202.2 8.3 %copy-start.3 = (bf16[512,1024]{0,1:T(8,128)(2,1)}, bf16[512,1024]{0,1:T(8,128)(2,1)S(1)}, u32[]{:S(2)}) copy-start(bf16[512,1024]{0,1:T(8,128)(2,1)S(1)} %get-tuple-element.15) | copy-start | bytes 3145732
  202.8 1.8 copy-start.11
  204.6 5.9 %copy-start.10 = (pred[512,1024]{1,0:T(8,128)(4,1)S(1)}, pred[512,1024]{1,0:T(8,128)(4,1)}, u32[]{:S(2)}) copy-start(pred[512,1024]{1,0:T(8,128)(4,1)} %iota_compare_fusion) | copy-start | bytes 1572868
  210.5 2.6 copy-start.5
  213.1 8.9 %copy-start.2 = (bf16[8,512,1024]{2,1,0:T(8,128)(2,1)}, bf16[8,512,1024]{2,1,0:T(8,128)(2,1)S(1)}, u32[]{:S(2)}) copy-start(bf16[8,512,1024]{2,1,0:T(8,128)(2,1)S(1)} %select_convert_fusion.2) | copy-start | bytes 25165828
  213.2 8.9 %copy-start.9 = (f32[8,128,512]{1,2,0:T(8,128)S(1)}, f32[8,128,512]{1,2,0:T(8,128)}, u32[]{:S(2)}) copy-start(f32[8,128,512]{1,2,0:T(8,128)} %fusion.57) | copy-start | bytes 6291460
  259.5 2.2 copy-start.1
Sparse Core Ops, SparseCore 0:
  9.6 152.3 all-gather.5
  164.4 34.7 all-gather.7
  201.1 36.5 all-gather.9
where the time goes:
time: 290 us; the launch traced here: 289 us
  waiting for transfers between devices  163 us (56%)
  matrix products  77 us (27%)
  local copies, waits for them, and re-layouts  26.2 us (9%)
  between operations  13.9 us (5%)
  other arithmetic  9.18 us (3%)
    all_gather x1, waiting for transfers between devices, local(): lax.all_gather(layer_grad, 'tp', axis=1, tiled=True)  150 us
    dot_general x2, matrix products, local(): jnp.einsum('kzx,zkm->xkm', inside_query, gradient_block, preferred_elemen...  15.7 us
    unnamed x27, local copies, waits for them, and re-layouts  15.4 us
    dot_general x1, matrix products, local(): lax.dot_general(lax.all_gather(layer_grad, 'tp', axis=1, tiled=True), out...  13.9 us
    dot_general x2, matrix products, local(): jnp.einsum('cxd,xcr->dcr', inside_gradient, query_blk, preferred_element_...  13.6 us
    all_gather x1, waiting for transfers between devices, local(): lax.all_gather(key_value_here[None], 'ctx', axis=0, tiled=True)  12.4 us
    dot_general x2, matrix products, local(): jnp.einsum('vmr,rve->mve', inside_gradient, key_three, preferred_element_...  11.5 us
    dot_general x2, matrix products, local(): jnp.einsum('thv,shv->hts', gradient_block, value_three, preferred_element...  8.52 us
  transfers between devices with their start and end apart: 3, of which 2 were waited for; matrix products, arithmetic and copies ran while one was open for 29% of the time, Pallas kernels for 0%

commit v1 on v0

v1 whole, which is shorter than its diff:
```python
import functools

import jax
import jax.numpy as jnp
from jax import lax
from jax.experimental import pallas as pl
from jax.experimental.pallas import tpu as pltpu
from jax.sharding import PartitionSpec as P

HEAD = 128
MESH = pl.DeviceIdType.MESH
F32 = jnp.float32
BF16 = jnp.bfloat16
NT = (((1,), (1,)), ((), ()))
NN = (((1,), (0,)), ((), ()))
TN = (((0,), (0,)), ((), ()))


def mm(a, b, dims):
    return lax.dot_general(a, b, dims, preferred_element_type=F32)


def attention_head(read, state_kv, state_grad, write, tokens, size, factor):
    count = tokens // size
    pieces = [read(i) for i in range(count)]
    rows = lax.broadcasted_iota(jnp.int32, (size, size), 0)
    cols = lax.broadcasted_iota(jnp.int32, (size, size), 1)
    causal = rows >= cols
    after = [None] * count
    total = state_grad
    for i in reversed(range(count)):
        after[i] = total.astype(BF16)
        if i:
            q, _, _, g = pieces[i]
            total = total + mm(q, g, TN)
    before = state_kv
    for i in range(count):
        q, k, v, g = pieces[i]
        inner_grad = jnp.where(causal, mm(g, v, NT), 0.0).astype(BF16)
        inner_query = jnp.where(causal, mm(q, k, NT), 0.0).astype(BF16)
        query = mm(inner_grad, k, NN) + mm(g, before.astype(BF16), NT)
        key = mm(inner_grad, q, TN) + mm(v, after[i], NT)
        value = mm(inner_query, g, TN) + mm(k, after[i], NN)
        write(i, (factor * query).astype(BF16), (factor * key).astype(BF16), (factor * value).astype(BF16))
        if i < count - 1:
            before = before + mm(k, v, TN)


def attention_kernel(size, factor, q_ref, k_ref, v_ref, g_ref, kv_ref, grad_ref, qo_ref, ko_ref, vo_ref):
    tokens = q_ref.shape[0]

    def read(i):
        at = pl.ds(i * size, size)
        return q_ref[at, :], k_ref[at, :], v_ref[at, :], g_ref[at, :]

    def write(i, query, key, value):
        at = pl.ds(i * size, size)
        qo_ref[at, :] = query
        ko_ref[at, :] = key
        vo_ref[at, :] = value

    attention_head(read, kv_ref[0].astype(F32), grad_ref[0].astype(F32), write, tokens, size, factor)


def attention(q, k, v, g, kv_before, grad_after, factor):
    tokens, columns = q.shape
    size = min(256, tokens)
    rows = pl.BlockSpec((tokens, HEAD), lambda h: (0, h))
    state = pl.BlockSpec((1, HEAD, HEAD), lambda h: (h, 0, 0))
    return pl.pallas_call(
        functools.partial(attention_kernel, size, factor),
        grid=(columns // HEAD,),
        out_shape=[jax.ShapeDtypeStruct(q.shape, BF16)] * 3,
        in_specs=[rows] * 4 + [state] * 2,
        out_specs=[rows] * 3,
    )(q, k, v, g, kv_before, grad_after)


def gather_kernel(
    n_ctx, q_hbm, k_hbm, v_hbm, lg_hbm, w_hbm, g_ref, kv_ref, grad_ref,
    q_buf, k_buf, v_buf, lg, w, far, part_out, part_in,
    kv_out, kv_in, grad_out, grad_in,
    load_sem, ends_sem, mids_sem, lg_recv, fwd_sem, part_sem, part_recv,
    far_sem, far_recv, twin_sem, twin_recv, kv_sem, kv_recv, grad_sem, grad_recv,
):
    me = lax.axis_index("ctx")
    z = lax.axis_index("tp")
    tokens, width = lg_hbm.shape
    columns = w_hbm.shape[0]
    heads = columns // HEAD
    chunks = lg_recv.shape[1]
    size = tokens // chunks
    pieces = far_sem.shape[0]
    half = columns // 2
    piece = half // pieces
    twin = me + 1 - 2 * (me % 2)
    core = me % 2
    is_end = (z == 0) | (z == 3)
    is_mid = (z == 1) | (z == 2)
    low = z // 2
    end = 3 * low
    mid = 1 + low
    mid2 = 2 - low
    end2 = 3 - end
    far_col = pl.multiple_of((1 - low) * 2 * width, 2 * width)
    near_col = pl.multiple_of(low * 2 * width, 2 * width)

    def col(part):
        return pl.ds(pl.multiple_of(part * width, width), width)

    def row(i):
        return pl.ds(pl.multiple_of(i * size, size), size)

    barrier = pltpu.get_barrier_semaphore()
    for d in range(1, n_ctx):
        pl.semaphore_signal(barrier, inc=1, device_id=((me + d) % n_ctx, z), device_id_type=MESH)

    @pl.when(is_end)
    def _():
        pl.semaphore_signal(barrier, inc=1, device_id=(me, mid), device_id_type=MESH)
        pl.semaphore_wait(barrier, n_ctx)

    @pl.when(is_mid)
    def _():
        pl.semaphore_signal(barrier, inc=1, device_id=(me, end), device_id_type=MESH)
        pl.semaphore_signal(barrier, inc=1, device_id=(me, mid2), device_id_type=MESH)
        pl.semaphore_wait(barrier, n_ctx + 1)

    def remote(src, dst, send, recv, target):
        return pltpu.make_async_remote_copy(
            src_ref=src, dst_ref=dst, send_sem=send, recv_sem=recv, device_id=target, device_id_type=MESH)

    def lg_from_hbm(i, sems, target_z):
        return remote(lg_hbm.at[row(i), :], lg.at[row(i), col(z)], sems.at[i], lg_recv.at[z, i], (me, target_z))

    def lg_forward(i):
        place = lg.at[row(i), col(end)]
        return remote(place, place, fwd_sem.at[i], lg_recv.at[end, i], (me, mid2))

    def lg_arrival(part, i):
        place = lg.at[row(i), col(part)]
        return remote(place, place, fwd_sem.at[i], lg_recv.at[part, i], (me, mid2))

    def far_rows(which, p):
        return pl.ds(pl.multiple_of(which * half + p * piece, piece), piece)

    def far_send(p):
        return remote(w_hbm.at[far_rows(core, p), pl.ds(far_col, 2 * width)], far.at[far_rows(core, p), :],
                      far_sem.at[p], far_recv.at[p], (me, mid))

    def far_share(p):
        place = far.at[far_rows(core, p), :]
        return remote(place, place, twin_sem.at[p], twin_recv.at[p], (twin, z))

    def far_twin(p):
        place = far.at[far_rows(1 - core, p), :]
        return remote(place, place, twin_sem.at[p], twin_recv.at[p], (twin, z))

    def part_send(i):
        return remote(part_out.at[row(i), :], part_in.at[row(i), :], part_sem.at[i], part_recv.at[i], (me, end))

    @pl.when(is_end)
    def _():
        for p in range(pieces):
            far_send(p).start()

        @pl.loop(0, chunks)
        def _(i):
            lg_from_hbm(i, ends_sem, mid).start()

    @pl.when(is_mid)
    def _():
        @pl.loop(0, chunks)
        def _(i):
            lg_from_hbm(i, ends_sem, end).start()
            lg_from_hbm(i, mids_sem, mid2).start()

    loads = [
        pltpu.make_async_copy(k_hbm, k_buf, load_sem.at[0]),
        pltpu.make_async_copy(v_hbm, v_buf, load_sem.at[1]),
        pltpu.make_async_copy(q_hbm, q_buf, load_sem.at[2]),
        pltpu.make_async_copy(lg_hbm, lg.at[:, col(z)], load_sem.at[3]),
        pltpu.make_async_copy(w_hbm, w, load_sem.at[4]),
    ]
    for load in loads:
        load.start()
    loads[0].wait()
    loads[1].wait()

    def head(h):
        return pl.ds(pl.multiple_of(h * HEAD, HEAD), HEAD)

    @pl.loop(0, heads)
    def _(h):
        kv_out[h] = mm(k_buf[:, head(h)], v_buf[:, head(h)], TN).astype(BF16)

    for d in range(1, n_ctx):
        @pl.when(me + d < n_ctx)
        def _():
            remote(kv_out, kv_in.at[d - 1], kv_sem.at[d - 1], kv_recv.at[d - 1], ((me + d) % n_ctx, z)).start()
    for load in loads[2:]:
        load.wait()

    tile = min(256, columns)

    @pl.when(is_end)
    def _():
        @pl.loop(0, chunks)
        def _(i):
            lg_arrival(mid, i).wait_recv()
            part_send(i).wait_recv()

            @pl.loop(0, columns // tile)
            def _(n):
                out = pl.ds(pl.multiple_of(n * tile, tile), tile)
                near = pl.ds(near_col, 2 * width)
                total = mm(lg[row(i), near], w[out, near], NT)
                g_ref[row(i), out] = (total + part_in[row(i), out].astype(F32)).astype(BF16)

    @pl.when(is_mid)
    def _():
        for p in range(pieces):
            far_send(p).wait_recv()
            far_share(p).start()
        lg_arrival(end, 0).wait_recv()
        lg_forward(0).start()
        for p in range(pieces):
            far_twin(p).wait_recv()

        @pl.loop(0, chunks)
        def _(i):
            @pl.when(i < chunks - 1)
            def _():
                lg_arrival(end, i + 1).wait_recv()
                lg_forward(i + 1).start()

            lg_arrival(mid2, i).wait_recv()
            lg_arrival(end2, i).wait_recv()

            @pl.loop(0, columns // tile)
            def _(n):
                out = pl.ds(pl.multiple_of(n * tile, tile), tile)
                part_out[row(i), out] = mm(lg[row(i), pl.ds(far_col, 2 * width)], far[out, :], NT).astype(BF16)

            part_send(i).start()

            @pl.loop(0, columns // tile)
            def _(n):
                out = pl.ds(pl.multiple_of(n * tile, tile), tile)
                g_ref[row(i), out] = mm(lg[row(i), :], w[out, :], NT).astype(BF16)

    @pl.loop(0, heads)
    def _(h):
        grad_out[h] = mm(q_buf[:, head(h)], g_ref[:, head(h)], TN).astype(BF16)

    for d in range(1, n_ctx):
        @pl.when(me >= d)
        def _():
            remote(grad_out, grad_in.at[d - 1], grad_sem.at[d - 1], grad_recv.at[d - 1], ((me + n_ctx - d) % n_ctx, z)).start()

    def add_up(source, recv, send, target, out_ref, wanted):
        for d in range(1, n_ctx):
            @pl.when(wanted(d))
            def _(d=d):
                remote(source.at[d - 1], source.at[d - 1], send.at[d - 1], recv.at[d - 1], (target, z)).wait_recv()

            @pl.when(jnp.logical_not(wanted(d)))
            def _(d=d):
                source[d - 1] = jnp.zeros(source.shape[1:], BF16)

        @pl.loop(0, heads)
        def _(h):
            total = source[0, h].astype(F32)
            for d in range(2, n_ctx):
                total = total + source[d - 1, h].astype(F32)
            out_ref[h] = total.astype(BF16)

    add_up(kv_in, kv_recv, kv_sem, twin, kv_ref, lambda d: me >= d)
    add_up(grad_in, grad_recv, grad_sem, twin, grad_ref, lambda d: me + d < n_ctx)

    for d in range(1, n_ctx):
        @pl.when(me + d < n_ctx)
        def _():
            remote(kv_out, kv_in.at[d - 1], kv_sem.at[d - 1], kv_recv.at[d - 1], (twin, z)).wait_send()

        @pl.when(me >= d)
        def _():
            remote(grad_out, grad_in.at[d - 1], grad_sem.at[d - 1], grad_recv.at[d - 1], (twin, z)).wait_send()

    @pl.when(is_end)
    def _():
        for p in range(pieces):
            far_send(p).wait_send()

        @pl.loop(0, chunks)
        def _(i):
            lg_from_hbm(i, ends_sem, mid).wait_send()

    @pl.when(is_mid)
    def _():
        for p in range(pieces):
            far_share(p).wait_send()

        @pl.loop(0, chunks)
        def _(i):
            lg_from_hbm(i, ends_sem, end).wait_send()
            lg_from_hbm(i, mids_sem, mid2).wait_send()
            lg_forward(i).wait_send()
            part_send(i).wait_send()


def gather(q, k, v, lg, w, n_ctx):
    tokens, width = lg.shape
    columns = w.shape[0]
    heads = columns // HEAD
    chunks = 8 if tokens % 128 == 0 and tokens >= 1024 else 1
    pieces = 4
    dma = pltpu.SemaphoreType.DMA
    state = (heads, HEAD, HEAD)
    slots = (n_ctx - 1,) + state
    any_spec = pl.BlockSpec(memory_space=pl.ANY)
    vmem_spec = pl.BlockSpec(memory_space=pltpu.VMEM)
    return pl.pallas_call(
        functools.partial(gather_kernel, n_ctx),
        out_shape=[
            jax.ShapeDtypeStruct((tokens, columns), BF16),
            jax.ShapeDtypeStruct(state, BF16),
            jax.ShapeDtypeStruct(state, BF16),
        ],
        in_specs=[any_spec] * 5,
        out_specs=[vmem_spec] * 3,
        scratch_shapes=[
            pltpu.VMEM((tokens, columns), BF16),
            pltpu.VMEM((tokens, columns), BF16),
            pltpu.VMEM((tokens, columns), BF16),
            pltpu.VMEM((tokens, 4 * width), BF16),
            pltpu.VMEM(w.shape, BF16),
            pltpu.VMEM((columns, 2 * width), BF16),
            pltpu.VMEM((tokens, columns), BF16),
            pltpu.VMEM((tokens, columns), BF16),
            pltpu.VMEM(state, BF16),
            pltpu.VMEM(slots, BF16),
            pltpu.VMEM(state, BF16),
            pltpu.VMEM(slots, BF16),
            dma((5,)), dma((chunks,)), dma((chunks,)), dma((4, chunks)), dma((chunks,)),
            dma((chunks,)), dma((chunks,)),
            dma((pieces,)), dma((pieces,)), dma((pieces,)), dma((pieces,)),
            dma((n_ctx - 1,)), dma((n_ctx - 1,)), dma((n_ctx - 1,)), dma((n_ctx - 1,)),
        ],
        compiler_params=pltpu.CompilerParams(
            collective_id=0, has_side_effects=True, vmem_limit_bytes=60 * 1024 * 1024),
    )(q, k, v, lg, w)


def gather_plain(q, k, v, lg, w):
    tokens, columns = q.shape
    heads = columns // HEAD
    me = lax.axis_index("ctx")
    g = lax.dot_general(lax.all_gather(lg, "tp", axis=1, tiled=True), w, NT, preferred_element_type=F32).astype(BF16)
    three = (tokens, heads, HEAD)
    kv_here = jnp.einsum("lbg,lbz->bgz", k.reshape(three), v.reshape(three), preferred_element_type=F32)
    grad_here = jnp.einsum("lbg,lbz->bgz", q.reshape(three), g.reshape(three), preferred_element_type=F32)

    def pick(mine, lower):
        stacked = lax.all_gather(mine[None], "ctx", axis=0, tiled=True)
        index = jnp.arange(stacked.shape[0])
        chosen = index < me if lower else index > me
        return jnp.sum(jnp.where(chosen[:, None, None, None], stacked, 0.0), 0).astype(BF16)

    return g, pick(kv_here, True), pick(grad_here, False)


def local(q, k, v, lg, w):
    n_ctx = lax.axis_size("ctx")
    n_tp = lax.axis_size("tp")
    factor = float((HEAD * q.shape[0] * n_ctx) ** (-0.5))
    if n_tp == 4 and n_ctx % 2 == 0:
        g, kv_before, grad_after = gather(q, k, v, lg, w, n_ctx)
    else:
        g, kv_before, grad_after = gather_plain(q, k, v, lg, w)
    return tuple(attention(q, k, v, g, kv_before, grad_after, factor))


def solution(mesh):
    return jax.shard_map(
        local,
        mesh=mesh,
        in_specs=(P("ctx", "tp"), P("ctx", "tp"), P("ctx", "tp"), P("ctx", "tp"), P("tp", None)),
        out_specs=(P("ctx", "tp"), P("ctx", "tp"), P("ctx", "tp")),
        check_vma=False,
    )
```

time: 290 us -> 158 us (0.54)
  waiting for transfers between devices: 163 us -> 0 us
  Pallas kernels: 0 us -> 157 us
  matrix products: 77 us -> 0 us
  local copies, waits for them, and re-layouts: 26.2 us -> 0 us
  between operations: 13.9 us -> 0.64 us
  other arithmetic: 9.18 us -> 0 us
    all_gather x3 -> x0, waiting for transfers between devices: 162 us -> none  [the longest x1 150 us: local(): lax.all_gather(layer_grad, 'tp', axis=1, tiled=True)]
    pallas_call x0 -> x2, Pallas kernels: none -> 157 us  [the longest x1 142 us: gather(): pl.pallas_call(functools.partial(gather_kernel, n_ctx), out_shape=[jax.Sh...]
    dot_general x15 -> x0, matrix products: 77 us -> none  [the longest x2 15.7 us: local(): jnp.einsum('kzx,zkm->xkm', inside_query, gradient_block, preferred_elemen...]
    unnamed x27 -> x0, local copies, waits for them, and re-layouts: 15.4 us -> none
    slice x4 -> x0, local copies, waits for them, and re-layouts: 5.87 us -> none  [the longest x3 5.71 us: local(): query_blk = query_three[begin_row:begin_row + block_len]]
    reduce_sum x2 -> x0, other arithmetic: 5.55 us -> none  [pick_sum(): jnp.sum(jnp.where(chosen[:, None, None, None], stacked, jnp.float32(0.0))...]
    concatenate x1 -> x0, local copies, waits for them, and re-layouts: 3.91 us -> none  [local(): query_grad = jnp.concatenate(query_parts, 0).reshape(tokens, columns)]
  transfers between devices with their start and end apart: 3 -> 0, of which waited for: 2 -> 0; matrix products, arithmetic and copies ran while one was open for 29% -> 0% of each run, Pallas kernels for 0% -> 0%
where the time goes in v1:
time: 158 us
  Pallas kernels  157 us (99%)
    pallas_call x1, Pallas kernels, gather(): pl.pallas_call(functools.partial(gather_kernel, n_ctx), out_shape=[jax.Sh...  142 us
    pallas_call x1, Pallas kernels, attention(): pl.pallas_call(functools.partial(attention_kernel, size, factor), grid=(c...  15.2 us

profile of v1, /device:TPU:0, one launch (start us, length us, event | category | flops | bytes accessed | tf_op | source)
XLA Modules:
  0.0 157.7 jit_solution(10523345949408462366)
XLA Ops:
  0.6 141.8 %shard_map.76 = (bf16[1024,1024]{1,0:T(8,128)(2,1)}, bf16[8,128,128]{2,1,0:T(8,128)(2,1)}, bf16[8,128,128]{2,1,0:T(8,128)(2,1)}) custom-call(bf16[1024,1024]{1,0:T(8,128)(2,1)} %q_ref.1, bf16[1024,1024]{1,0:T(8,128)(2,1)} %k_ref.1, bf16[1024,1024]{1,0:T(8,128)(2,1)} %v_ref.1, bf16[1024,1024]{1,0:T(8,128)(2,1)} %lg_hbm.1, bf16[1024,4096]{1,0:T(8,128)(2,1)} %w_hbm.1), custom_call_target="tpu_custom_call" | custom-call | tf_op jit(solution)/shard_map/pallas_call | solution.py:323
  142.4 15.2 %shard_map.77 = (bf16[1024,1024]{1,0:T(8,128)(2,1)}, bf16[1024,1024]{1,0:T(8,128)(2,1)}, bf16[1024,1024]{1,0:T(8,128)(2,1)}) custom-call(bf16[1024,1024]{1,0:T(8,128)(2,1)} %q_ref.1, bf16[1024,1024]{1,0:T(8,128)(2,1)} %k_ref.1, bf16[1024,1024]{1,0:T(8,128)(2,1)} %v_ref.1, bf16[1024,1024]{1,0:T(8,128)(2,1)} %get-tuple-element.6.g_ref, ...), custom_call_target="tpu_custom_call" | custom-call | tf_op jit(solution)/shard_map/pallas_call | solution.py:70

commit v2 on v1

--- a/solution.py
+++ b/solution.py
@@ -77,11 +77,12 @@
 
 
 def gather_kernel(
-    n_ctx, q_hbm, k_hbm, v_hbm, lg_hbm, w_hbm, g_ref, kv_ref, grad_ref,
-    q_buf, k_buf, v_buf, lg, w, far, part_out, part_in,
-    kv_out, kv_in, grad_out, grad_in,
+    n_ctx, factor, q_hbm, k_hbm, v_hbm, lg_hbm, w_hbm, qo_hbm, ko_hbm, vo_hbm,
+    q_buf, k_buf, v_buf, g_ref, lg, w, far, part_out, part_in,
+    qo_buf, ko_buf, vo_buf, key_part, value_part, kv_sums, kv_state, grad_sums, after,
+    kv_out, kv_in, grad_out, grad_twin, pair, pair_in, rest, rest_in,
     load_sem, ends_sem, mids_sem, lg_recv, fwd_sem, part_sem, part_recv,
-    far_sem, far_recv, twin_sem, twin_recv, kv_sem, kv_recv, grad_sem, grad_recv,
+    far_sem, far_recv, twin_sem, twin_recv, kv_sem, kv_recv, pair_sem, pair_recv, core_sem, core_recv, out_sem,
 ):
     me = lax.axis_index("ctx")
     z = lax.axis_index("tp")
@@ -190,9 +191,25 @@
     def head(h):
         return pl.ds(pl.multiple_of(h * HEAD, HEAD), HEAD)
 
+    blocks = kv_sums.shape[0]
+    block = tokens // blocks
+    per = chunks // blocks
+    half_heads = heads // 2
+    rows_at = lax.broadcasted_iota(jnp.int32, (block, block), 0)
+    cols_at = lax.broadcasted_iota(jnp.int32, (block, block), 1)
+    causal = rows_at >= cols_at
+
+    def span(c):
+        return pl.ds(pl.multiple_of(c * block, block), block)
+
     @pl.loop(0, heads)
     def _(h):
-        kv_out[h] = mm(k_buf[:, head(h)], v_buf[:, head(h)], TN).astype(BF16)
+        total = jnp.zeros((HEAD, HEAD), F32)
+        for c in range(blocks):
+            here = mm(k_buf[span(c), head(h)], v_buf[span(c), head(h)], TN)
+            kv_sums[c, h] = here
+            total = total + here
+        kv_out[h] = total.astype(BF16)
 
     for d in range(1, n_ctx):
         @pl.when(me + d < n_ctx)
@@ -203,8 +220,55 @@
 
     tile = min(256, columns)
 
+    def finish_kv():
+        for d in range(1, n_ctx):
+            @pl.when(me >= d)
+            def _():
+                remote(kv_in.at[d - 1], kv_in.at[d - 1], kv_sem.at[d - 1], kv_recv.at[d - 1], (twin, z)).wait_recv()
+
+            @pl.when(me < d)
+            def _():
+                kv_in[d - 1] = jnp.zeros(kv_in.shape[1:], BF16)
+
+        @pl.loop(0, heads)
+        def _(h):
+            total = kv_in[0, h].astype(F32)
+            for d in range(2, n_ctx):
+                total = total + kv_in[d - 1, h].astype(F32)
+            for c in range(blocks):
+                kv_state[c, h] = total.astype(BF16)
+                total = total + kv_sums[c, h]
+
+    def attend(c, h):
+        at, hd = span(c), head(h)
+        q, k, v, g = q_buf[at, hd], k_buf[at, hd], v_buf[at, hd], g_ref[at, hd]
+        inner_grad = jnp.where(causal, mm(g, v, NT), 0.0).astype(BF16)
+        inner_query = jnp.where(causal, mm(q, k, NT), 0.0).astype(BF16)
+        query = mm(inner_grad, k, NN) + mm(g, kv_state[c, h], NT)
+        qo_buf[at, hd] = (factor * query).astype(BF16)
+        key_part[at, hd] = mm(inner_grad, q, TN)
+        value_part[at, hd] = mm(inner_query, g, TN)
+
+    def attend_step(i):
+        @pl.when(i >= per)
+        def _():
+            share = heads // per
+
+            @pl.loop(0, share)
+            def _(j):
+                attend(i // per - 1, (i % per) * share + j)
+
+        @pl.when(i % per == per - 1)
+        def _():
+            @pl.loop(0, heads)
+            def _(h):
+                c = i // per
+                grad_sums[c, h] = mm(q_buf[span(c), head(h)], g_ref[span(c), head(h)], TN)
+
     @pl.when(is_end)
     def _():
+        finish_kv()
+
         @pl.loop(0, chunks)
         def _(i):
             lg_arrival(mid, i).wait_recv()
@@ -217,11 +281,14 @@
                 total = mm(lg[row(i), near], w[out, near], NT)
                 g_ref[row(i), out] = (total + part_in[row(i), out].astype(F32)).astype(BF16)
 
+            attend_step(i)
+
     @pl.when(is_mid)
     def _():
         for p in range(pieces):
             far_send(p).wait_recv()
             far_share(p).start()
+        finish_kv()
         lg_arrival(end, 0).wait_recv()
         lg_forward(0).start()
         for p in range(pieces):
@@ -249,43 +316,125 @@
                 out = pl.ds(pl.multiple_of(n * tile, tile), tile)
                 g_ref[row(i), out] = mm(lg[row(i), :], w[out, :], NT).astype(BF16)
 
+            attend_step(i)
+
+    chip = me // 2
+    n_chips = n_ctx // 2
+    mine = pl.ds(pl.multiple_of(core * half_heads, half_heads), half_heads)
+    other = pl.ds(pl.multiple_of((1 - core) * half_heads, half_heads), half_heads)
+
     @pl.loop(0, heads)
     def _(h):
-        grad_out[h] = mm(q_buf[:, head(h)], g_ref[:, head(h)], TN).astype(BF16)
-
-    for d in range(1, n_ctx):
-        @pl.when(me >= d)
-        def _():
-            remote(grad_out, grad_in.at[d - 1], grad_sem.at[d - 1], grad_recv.at[d - 1], ((me + n_ctx - d) % n_ctx, z)).start()
-
-    def add_up(source, recv, send, target, out_ref, wanted):
-        for d in range(1, n_ctx):
-            @pl.when(wanted(d))
-            def _(d=d):
-                remote(source.at[d - 1], source.at[d - 1], send.at[d - 1], recv.at[d - 1], (target, z)).wait_recv()
-
-            @pl.when(jnp.logical_not(wanted(d)))
-            def _(d=d):
-                source[d - 1] = jnp.zeros(source.shape[1:], BF16)
-
+        total = grad_sums[0, h]
+        for c in range(1, blocks):
+            total = total + grad_sums[c, h]
+        after[h] = total
+        grad_out[h] = total.astype(BF16)
+
+    swap = remote(grad_out.at[other], grad_twin.at[other], core_sem.at[0], core_recv.at[0], (twin, z))
+    swap_in = remote(grad_out.at[mine], grad_twin.at[mine], core_sem.at[0], core_recv.at[0], (twin, z))
+    extra = remote(grad_out.at[mine], grad_twin.at[mine], core_sem.at[1], core_recv.at[1], (twin, z))
+    extra_in = remote(grad_out.at[other], grad_twin.at[other], core_sem.at[1], core_recv.at[1], (twin, z))
+    swap.start()
+
+    @pl.when(core == 1)
+    def _():
+        extra.start()
+
+    swap_in.wait_recv()
+
+    @pl.loop(0, half_heads)
+    def _(j):
+        h = core * half_heads + j
+        pair[j] = (after[h] + grad_twin[h].astype(F32)).astype(BF16)
+
+    def pair_copy(d):
+        return remote(pair, pair_in.at[d - 1], pair_sem.at[d - 1], pair_recv.at[d - 1],
+                      ((me + n_ctx - 2 * d) % n_ctx, z))
+
+    for d in range(1, n_chips):
+        @pl.when(chip >= d)
+        def _():
+            pair_copy(d).start()
+
+    @pl.loop(0, heads)
+    def _(h):
+        attend(blocks - 1, h)
+
+    query_out = pltpu.make_async_copy(qo_buf, qo_hbm, out_sem.at[2 * blocks])
+    query_out.start()
+
+    for d in range(1, n_chips):
+        @pl.when(chip + d < n_chips)
+        def _():
+            pair_copy(d).wait_recv()
+
+        @pl.when(chip + d >= n_chips)
+        def _():
+            pair_in[d - 1] = jnp.zeros(pair_in.shape[1:], BF16)
+
+    @pl.loop(0, half_heads)
+    def _(j):
+        total = pair_in[0, j].astype(F32)
+        for d in range(2, n_chips):
+            total = total + pair_in[d - 1, j].astype(F32)
+        rest[j] = total
+
+    last = remote(rest, rest_in, core_sem.at[2], core_recv.at[2], (twin, z))
+    last.start()
+
+    @pl.when(core == 0)
+    def _():
+        extra_in.wait_recv()
+
+    last.wait_recv()
+
+    @pl.loop(0, half_heads)
+    def _(j):
+        after[core * half_heads + j] = rest[j]
+        after[(1 - core) * half_heads + j] = rest_in[j]
+
+    @pl.when(core == 0)
+    def _():
         @pl.loop(0, heads)
         def _(h):
-            total = source[0, h].astype(F32)
-            for d in range(2, n_ctx):
-                total = total + source[d - 1, h].astype(F32)
-            out_ref[h] = total.astype(BF16)
-
-    add_up(kv_in, kv_recv, kv_sem, twin, kv_ref, lambda d: me >= d)
-    add_up(grad_in, grad_recv, grad_sem, twin, grad_ref, lambda d: me + d < n_ctx)
+            after[h] = after[h] + grad_twin[h].astype(F32)
+
+    outs = []
+    for c in reversed(range(blocks)):
+        at = pl.ds(c * block, block)
+
+        @pl.loop(0, heads)
+        def _(h):
+            state = after[h]
+            low_state = state.astype(BF16)
+            key = key_part[at, head(h)] + mm(v_buf[at, head(h)], low_state, NT)
+            value = value_part[at, head(h)] + mm(k_buf[at, head(h)], low_state, NN)
+            ko_buf[at, head(h)] = (factor * key).astype(BF16)
+            vo_buf[at, head(h)] = (factor * value).astype(BF16)
+            after[h] = state + grad_sums[c, h]
+
+        outs.append(pltpu.make_async_copy(ko_buf.at[at, :], ko_hbm.at[at, :], out_sem.at[c]))
+        outs.append(pltpu.make_async_copy(vo_buf.at[at, :], vo_hbm.at[at, :], out_sem.at[blocks + c]))
+        outs[-2].start()
+        outs[-1].start()
+
+    swap.wait_send()
+    last.wait_send()
+
+    @pl.when(core == 1)
+    def _():
+        extra.wait_send()
 
     for d in range(1, n_ctx):
         @pl.when(me + d < n_ctx)
         def _():
             remote(kv_out, kv_in.at[d - 1], kv_sem.at[d - 1], kv_recv.at[d - 1], (twin, z)).wait_send()
 
-        @pl.when(me >= d)
-        def _():
-            remote(grad_out, grad_in.at[d - 1], grad_sem.at[d - 1], grad_recv.at[d - 1], (twin, z)).wait_send()
+    for d in range(1, n_chips):
+        @pl.when(chip >= d)
+        def _():
+            pair_copy(d).wait_send()
 
     @pl.when(is_end)
     def _():
@@ -308,47 +457,46 @@
             lg_forward(i).wait_send()
             part_send(i).wait_send()
 
-
-def gather(q, k, v, lg, w, n_ctx):
+    query_out.wait()
+    for out in outs:
+        out.wait()
+
+
+def fused(q, k, v, lg, w, n_ctx, factor):
     tokens, width = lg.shape
     columns = w.shape[0]
     heads = columns // HEAD
-    chunks = 8 if tokens % 128 == 0 and tokens >= 1024 else 1
+    chunks = 8
+    blocks = 4
     pieces = 4
     dma = pltpu.SemaphoreType.DMA
+    vmem = pltpu.VMEM
     state = (heads, HEAD, HEAD)
-    slots = (n_ctx - 1,) + state
+    half = (heads // 2, HEAD, HEAD)
+    whole = (tokens, columns)
+    chips = n_ctx // 2
     any_spec = pl.BlockSpec(memory_space=pl.ANY)
-    vmem_spec = pl.BlockSpec(memory_space=pltpu.VMEM)
     return pl.pallas_call(
-        functools.partial(gather_kernel, n_ctx),
-        out_shape=[
-            jax.ShapeDtypeStruct((tokens, columns), BF16),
-            jax.ShapeDtypeStruct(state, BF16),
-            jax.ShapeDtypeStruct(state, BF16),
-        ],
+        functools.partial(gather_kernel, n_ctx, factor),
+        out_shape=[jax.ShapeDtypeStruct(whole, BF16)] * 3,
         in_specs=[any_spec] * 5,
-        out_specs=[vmem_spec] * 3,
+        out_specs=[any_spec] * 3,
         scratch_shapes=[
-            pltpu.VMEM((tokens, columns), BF16),
-            pltpu.VMEM((tokens, columns), BF16),
-            pltpu.VMEM((tokens, columns), BF16),
-            pltpu.VMEM((tokens, 4 * width), BF16),
-            pltpu.VMEM(w.shape, BF16),
-            pltpu.VMEM((columns, 2 * width), BF16),
-            pltpu.VMEM((tokens, columns), BF16),
-            pltpu.VMEM((tokens, columns), BF16),
-            pltpu.VMEM(state, BF16),
-            pltpu.VMEM(slots, BF16),
-            pltpu.VMEM(state, BF16),
-            pltpu.VMEM(slots, BF16),
+            vmem(whole, BF16), vmem(whole, BF16), vmem(whole, BF16), vmem(whole, BF16),
+            vmem((tokens, 4 * width), BF16), vmem(w.shape, BF16), vmem((columns, 2 * width), BF16),
+            vmem(whole, BF16), vmem(whole, BF16),
+            vmem(whole, BF16), vmem(whole, BF16), vmem(whole, BF16), vmem(whole, F32), vmem(whole, F32),
+            vmem((blocks,) + state, F32), vmem((blocks,) + state, BF16), vmem((blocks,) + state, F32), vmem(state, F32),
+            vmem(state, BF16), vmem((n_ctx - 1,) + state, BF16), vmem(state, BF16), vmem(state, BF16),
+            vmem(half, BF16), vmem((chips - 1,) + half, BF16), vmem(half, F32), vmem(half, F32),
             dma((5,)), dma((chunks,)), dma((chunks,)), dma((4, chunks)), dma((chunks,)),
             dma((chunks,)), dma((chunks,)),
             dma((pieces,)), dma((pieces,)), dma((pieces,)), dma((pieces,)),
-            dma((n_ctx - 1,)), dma((n_ctx - 1,)), dma((n_ctx - 1,)), dma((n_ctx - 1,)),
+            dma((n_ctx - 1,)), dma((n_ctx - 1,)), dma((chips - 1,)), dma((chips - 1,)),
+            dma((3,)), dma((3,)), dma((2 * blocks + 1,)),
         ],
         compiler_params=pltpu.CompilerParams(
-            collective_id=0, has_side_effects=True, vmem_limit_bytes=60 * 1024 * 1024),
+            collective_id=0, has_side_effects=True, vmem_limit_bytes=62 * 1024 * 1024),
     )(q, k, v, lg, w)
 
 
@@ -374,10 +522,9 @@
     n_ctx = lax.axis_size("ctx")
     n_tp = lax.axis_size("tp")
     factor = float((HEAD * q.shape[0] * n_ctx) ** (-0.5))
-    if n_tp == 4 and n_ctx % 2 == 0:
-        g, kv_before, grad_after = gather(q, k, v, lg, w, n_ctx)
-    else:
-        g, kv_before, grad_after = gather_plain(q, k, v, lg, w)
+    if n_tp == 4 and n_ctx % 2 == 0 and n_ctx > 2 and q.shape[0] % 1024 == 0 and q.shape[1] % 256 == 0:
+        return tuple(fused(q, k, v, lg, w, n_ctx, factor))
+    g, kv_before, grad_after = gather_plain(q, k, v, lg, w)
     return tuple(attention(q, k, v, g, kv_before, grad_after, factor))
 
 

time: 158 us -> 156 us (0.987)
  Pallas kernels: 157 us -> 149 us
  local copies, waits for them, and re-layouts: 0 us -> 6.9 us
    pallas_call x2 -> x1, Pallas kernels: 157 us -> 149 us  [fused(): pl.pallas_call(functools.partial(gather_kernel, n_ctx, factor), out_shape...]
    unnamed x0 -> x7, local copies, waits for them, and re-layouts: none -> 6.9 us
where the time goes in v2:
time: 156 us
  Pallas kernels  149 us (96%)
  local copies, waits for them, and re-layouts  6.9 us (4%)
    pallas_call x1, Pallas kernels, fused(): pl.pallas_call(functools.partial(gather_kernel, n_ctx, factor), out_shape...  149 us
    unnamed x7, local copies, waits for them, and re-layouts  6.9 us

profile of v2, /device:TPU:0, one launch (start us, length us, event | category | flops | bytes accessed | tf_op | source)
XLA Modules:
  0.0 156.3 jit_solution(17848407606588542175)
XLA Ops:
  0.6 148.7 %shard_map.76 = (bf16[1024,1024]{1,0:T(8,128)(2,1)}, bf16[1024,1024]{1,0:T(8,128)(2,1)}, bf16[1024,1024]{1,0:T(8,128)(2,1)}) custom-call(bf16[1024,1024]{1,0:T(8,128)(2,1)} %q_hbm.1, bf16[1024,1024]{1,0:T(8,128)(2,1)} %k_hbm.1, bf16[1024,1024]{1,0:T(8,128)(2,1)} %v_hbm.1, bf16[1024,1024]{1,0:T(8,128)(2,1)} %lg_hbm.1, bf16[1024,4096]{1,0:T(8,128)(2,1)} %w_hbm.1), custom_call_target="tpu_custom_call" | custom-call | tf_op jit(solution)/shard_map/pallas_call | solution.py:479
  149.4 0.0 copy-start.1
  149.4 3.2 %copy.11 = bf16[1024,1024]{1,0:T(8,128)(2,1)} copy(bf16[1024,1024]{1,0:T(8,128)(2,1)} %get-tuple-element.6) | data formatting | bytes 4194304
  152.6 0.0 copy-done.1
  152.6 0.0 copy-start
  152.6 1.3 copy.12
  153.9 1.0 copy-done
  155.0 1.3 copy.13
Async XLA Ops:
  149.4 3.2 %copy-start.1 = (bf16[1024,1024]{1,0:T(8,128)(2,1)S(1)}, bf16[1024,1024]{1,0:T(8,128)(2,1)}, u32[]{:S(2)}) copy-start(bf16[1024,1024]{1,0:T(8,128)(2,1)} %get-tuple-element.7) | copy-start | bytes 6291460
  152.6 2.3 %copy-start = (bf16[1024,1024]{1,0:T(8,128)(2,1)S(1)}, bf16[1024,1024]{1,0:T(8,128)(2,1)}, u32[]{:S(2)}) copy-start(bf16[1024,1024]{1,0:T(8,128)(2,1)} %get-tuple-element.8) | copy-start | bytes 6291460

commit v3 on v2

--- a/solution.py
+++ b/solution.py
@@ -258,6 +258,7 @@
             def _(j):
                 attend(i // per - 1, (i % per) * share + j)
 
+    def sum_step(i):
         @pl.when(i % per == per - 1)
         def _():
             @pl.loop(0, heads)
@@ -265,34 +266,51 @@
                 c = i // per
                 grad_sums[c, h] = mm(q_buf[span(c), head(h)], g_ref[span(c), head(h)], TN)
 
+    def project(left, right, out_ref, at):
+        @pl.loop(0, columns // tile)
+        def _(n):
+            out = pl.ds(pl.multiple_of(n * tile, tile), tile)
+            out_ref[at, out] = mm(left[at, :], right[out, :], NT)
+
+    near = pl.ds(near_col, 2 * width)
+    middle = pl.ds(width, 2 * width)
+    far_mid2 = pl.ds(pl.multiple_of(low * width, width), width)
+    far_end2 = pl.ds(pl.multiple_of((1 - low) * width, width), width)
+
     @pl.when(is_end)
     def _():
+        @pl.loop(0, blocks)
+        def _(c):
+            for j in range(per):
+                lg_arrival(mid, c * per + j).wait_recv()
+            project(lg.at[:, near], w.at[:, near], key_part, span(c))
+
         finish_kv()
 
         @pl.loop(0, chunks)
         def _(i):
-            lg_arrival(mid, i).wait_recv()
+            attend_step(i)
             part_send(i).wait_recv()
-
-            @pl.loop(0, columns // tile)
-            def _(n):
-                out = pl.ds(pl.multiple_of(n * tile, tile), tile)
-                near = pl.ds(near_col, 2 * width)
-                total = mm(lg[row(i), near], w[out, near], NT)
-                g_ref[row(i), out] = (total + part_in[row(i), out].astype(F32)).astype(BF16)
-
-            attend_step(i)
+            g_ref[row(i), :] = (key_part[row(i), :] + part_in[row(i), :].astype(F32)).astype(BF16)
+            sum_step(i)
 
     @pl.when(is_mid)
     def _():
-        for p in range(pieces):
-            far_send(p).wait_recv()
-            far_share(p).start()
-        finish_kv()
+        for c in range(blocks):
+            for j in range(per):
+                lg_arrival(mid2, c * per + j).wait_recv()
+            far_send(c).wait_recv()
+            far_share(c).start()
+            project(lg.at[:, middle], w.at[:, middle], key_part, span(c))
         lg_arrival(end, 0).wait_recv()
         lg_forward(0).start()
+        finish_kv()
         for p in range(pieces):
             far_twin(p).wait_recv()
+
+        @pl.loop(0, blocks)
+        def _(c):
+            project(lg.at[:, col(mid2)], far.at[:, far_mid2], value_part, span(c))
 
         @pl.loop(0, chunks)
         def _(i):
@@ -301,22 +319,24 @@
                 lg_arrival(end, i + 1).wait_recv()
                 lg_forward(i + 1).start()
 
-            lg_arrival(mid2, i).wait_recv()
+            attend_step(i)
             lg_arrival(end2, i).wait_recv()
 
             @pl.loop(0, columns // tile)
             def _(n):
                 out = pl.ds(pl.multiple_of(n * tile, tile), tile)
-                part_out[row(i), out] = mm(lg[row(i), pl.ds(far_col, 2 * width)], far[out, :], NT).astype(BF16)
+                total = value_part[row(i), out] + mm(lg[row(i), col(end2)], far[out, far_end2], NT)
+                part_out[row(i), out] = total.astype(BF16)
 
             part_send(i).start()
 
             @pl.loop(0, columns // tile)
             def _(n):
                 out = pl.ds(pl.multiple_of(n * tile, tile), tile)
-                g_ref[row(i), out] = mm(lg[row(i), :], w[out, :], NT).astype(BF16)
-
-            attend_step(i)
+                total = key_part[row(i), out] + mm(lg[row(i), col(end)], w[out, col(end)], NT)
+                g_ref[row(i), out] = (total + mm(lg[row(i), col(end2)], w[out, col(end2)], NT)).astype(BF16)
+
+            sum_step(i)
 
     chip = me // 2
     n_chips = n_ctx // 2

time: 156 us -> 142 us (0.910)
  Pallas kernels: 149 us -> 134 us
    pallas_call x1, Pallas kernels: 149 us -> 134 us  [fused(): pl.pallas_call(functools.partial(gather_kernel, n_ctx, factor), out_shape...]
where the time goes in v3:
time: 142 us
  Pallas kernels  134 us (94%)
  local copies, waits for them, and re-layouts  6.9 us (5%)
    pallas_call x1, Pallas kernels, fused(): pl.pallas_call(functools.partial(gather_kernel, n_ctx, factor), out_shape...  134 us
    unnamed x7, local copies, waits for them, and re-layouts  6.9 us

profile of v3, /device:TPU:0, one launch (start us, length us, event | category | flops | bytes accessed | tf_op | source)
XLA Modules:
  0.0 141.9 jit_solution(12152282332586983242)
XLA Ops:
  0.6 134.4 %shard_map.76 = (bf16[1024,1024]{1,0:T(8,128)(2,1)}, bf16[1024,1024]{1,0:T(8,128)(2,1)}, bf16[1024,1024]{1,0:T(8,128)(2,1)}) custom-call(bf16[1024,1024]{1,0:T(8,128)(2,1)} %q_hbm.1, bf16[1024,1024]{1,0:T(8,128)(2,1)} %k_hbm.1, bf16[1024,1024]{1,0:T(8,128)(2,1)} %v_hbm.1, bf16[1024,1024]{1,0:T(8,128)(2,1)} %lg_hbm.1, bf16[1024,4096]{1,0:T(8,128)(2,1)} %w_hbm.1), custom_call_target="tpu_custom_call" | custom-call | tf_op jit(solution)/shard_map/pallas_call | solution.py:499
  135.0 0.0 copy-start.1
  135.0 3.2 %copy.11 = bf16[1024,1024]{1,0:T(8,128)(2,1)} copy(bf16[1024,1024]{1,0:T(8,128)(2,1)} %get-tuple-element.6) | data formatting | bytes 4194304
  138.2 0.0 copy-done.1
  138.2 0.0 copy-start
  138.2 1.3 copy.12
  139.6 1.0 copy-done
  140.6 1.3 copy.13
Async XLA Ops:
  135.0 3.2 %copy-start.1 = (bf16[1024,1024]{1,0:T(8,128)(2,1)S(1)}, bf16[1024,1024]{1,0:T(8,128)(2,1)}, u32[]{:S(2)}) copy-start(bf16[1024,1024]{1,0:T(8,128)(2,1)} %get-tuple-element.7) | copy-start | bytes 6291460
  138.2 2.3 %copy-start = (bf16[1024,1024]{1,0:T(8,128)(2,1)S(1)}, bf16[1024,1024]{1,0:T(8,128)(2,1)}, u32[]{:S(2)}) copy-start(bf16[1024,1024]{1,0:T(8,128)(2,1)} %get-tuple-element.8) | copy-start | bytes 6291460

commit v4 on v3

--- a/solution.py
+++ b/solution.py
@@ -77,12 +77,12 @@
 
 
 def gather_kernel(
-    n_ctx, factor, q_hbm, k_hbm, v_hbm, lg_hbm, w_hbm, qo_hbm, ko_hbm, vo_hbm,
+    n_ctx, factor, q_hbm, k_hbm, v_hbm, lg_hbm, w_hbm, qo_buf, ko_buf, vo_buf,
     q_buf, k_buf, v_buf, g_ref, lg, w, far, part_out, part_in,
-    qo_buf, ko_buf, vo_buf, key_part, value_part, kv_sums, kv_state, grad_sums, after,
+    key_part, value_part, kv_sums, kv_state, grad_sums, after,
     kv_out, kv_in, grad_out, grad_twin, pair, pair_in, rest, rest_in,
     load_sem, ends_sem, mids_sem, lg_recv, fwd_sem, part_sem, part_recv,
-    far_sem, far_recv, twin_sem, twin_recv, kv_sem, kv_recv, pair_sem, pair_recv, core_sem, core_recv, out_sem,
+    far_sem, far_recv, twin_sem, twin_recv, kv_sem, kv_recv, pair_sem, pair_recv, core_sem, core_recv,
 ):
     me = lax.axis_index("ctx")
     z = lax.axis_index("tp")
@@ -92,10 +92,13 @@
     chunks = lg_recv.shape[1]
     size = tokens // chunks
     pieces = far_sem.shape[0]
-    half = columns // 2
-    piece = half // pieces
+    quarter = columns // 4
+    piece = quarter // pieces
+    share = me % 4
     twin = me + 1 - 2 * (me % 2)
     core = me % 2
+    pal = me + 2 - 4 * ((me // 2) % 2)
+    pal_share = (share + 2) % 4
     is_end = (z == 0) | (z == 3)
     is_mid = (z == 1) | (z == 2)
     low = z // 2
@@ -143,19 +146,15 @@
         return remote(place, place, fwd_sem.at[i], lg_recv.at[part, i], (me, mid2))
 
     def far_rows(which, p):
-        return pl.ds(pl.multiple_of(which * half + p * piece, piece), piece)
+        return pl.ds(pl.multiple_of(which * quarter + p * piece, piece), piece)
 
     def far_send(p):
-        return remote(w_hbm.at[far_rows(core, p), pl.ds(far_col, 2 * width)], far.at[far_rows(core, p), :],
+        return remote(w_hbm.at[far_rows(share, p), pl.ds(far_col, 2 * width)], far.at[far_rows(share, p), :],
                       far_sem.at[p], far_recv.at[p], (me, mid))
 
-    def far_share(p):
-        place = far.at[far_rows(core, p), :]
-        return remote(place, place, twin_sem.at[p], twin_recv.at[p], (twin, z))
-
-    def far_twin(p):
-        place = far.at[far_rows(1 - core, p), :]
-        return remote(place, place, twin_sem.at[p], twin_recv.at[p], (twin, z))
+    def far_share(which, p, slot, target):
+        place = far.at[far_rows(which, p), :]
+        return remote(place, place, twin_sem.at[slot, p], twin_recv.at[slot, p], (target, z))
 
     def part_send(i):
         return remote(part_out.at[row(i), :], part_in.at[row(i), :], part_sem.at[i], part_recv.at[i], (me, end))
@@ -194,6 +193,7 @@
     blocks = kv_sums.shape[0]
     block = tokens // blocks
     per = chunks // blocks
+    ahead = 3
     half_heads = heads // 2
     rows_at = lax.broadcasted_iota(jnp.int32, (block, block), 0)
     cols_at = lax.broadcasted_iota(jnp.int32, (block, block), 1)
@@ -299,14 +299,22 @@
         for c in range(blocks):
             for j in range(per):
                 lg_arrival(mid2, c * per + j).wait_recv()
-            far_send(c).wait_recv()
-            far_share(c).start()
+            if c < pieces:
+                far_send(c).wait_recv()
+                far_share(share, c, 0, pal).start()
+                far_share(share, c, 1, twin).start()
+            if c == pieces:
+                for p in range(pieces):
+                    far_share(pal_share, p, 0, pal).wait_recv()
+                    far_share(pal_share, p, 2, twin).start()
+            for i in {2: (0,), 3: (1, 2)}.get(c, ()):
+                lg_arrival(end, i).wait_recv()
+                lg_forward(i).start()
             project(lg.at[:, middle], w.at[:, middle], key_part, span(c))
-        lg_arrival(end, 0).wait_recv()
-        lg_forward(0).start()
         finish_kv()
         for p in range(pieces):
-            far_twin(p).wait_recv()
+            far_share(share + 1 - 2 * core, p, 1, twin).wait_recv()
+            far_share(pal_share + 1 - 2 * core, p, 2, twin).wait_recv()
 
         @pl.loop(0, blocks)
         def _(c):
@@ -314,10 +322,10 @@
 
         @pl.loop(0, chunks)
         def _(i):
-            @pl.when(i < chunks - 1)
+            @pl.when(i < chunks - ahead)
             def _():
-                lg_arrival(end, i + 1).wait_recv()
-                lg_forward(i + 1).start()
+                lg_arrival(end, i + ahead).wait_recv()
+                lg_forward(i + ahead).start()
 
             attend_step(i)
             lg_arrival(end2, i).wait_recv()
@@ -381,9 +389,6 @@
     def _(h):
         attend(blocks - 1, h)
 
-    query_out = pltpu.make_async_copy(qo_buf, qo_hbm, out_sem.at[2 * blocks])
-    query_out.start()
-
     for d in range(1, n_chips):
         @pl.when(chip + d < n_chips)
         def _():
@@ -420,7 +425,6 @@
         def _(h):
             after[h] = after[h] + grad_twin[h].astype(F32)
 
-    outs = []
     for c in reversed(range(blocks)):
         at = pl.ds(c * block, block)
 
@@ -434,11 +438,6 @@
             vo_buf[at, head(h)] = (factor * value).astype(BF16)
             after[h] = state + grad_sums[c, h]
 
-        outs.append(pltpu.make_async_copy(ko_buf.at[at, :], ko_hbm.at[at, :], out_sem.at[c]))
-        outs.append(pltpu.make_async_copy(vo_buf.at[at, :], vo_hbm.at[at, :], out_sem.at[blocks + c]))
-        outs[-2].start()
-        outs[-1].start()
-
     swap.wait_send()
     last.wait_send()
 
@@ -468,7 +467,9 @@
     @pl.when(is_mid)
     def _():
         for p in range(pieces):
-            far_share(p).wait_send()
+            far_share(share, p, 0, pal).wait_send()
+            far_share(share, p, 1, twin).wait_send()
+            far_share(pal_share, p, 2, twin).wait_send()
 
         @pl.loop(0, chunks)
         def _(i):
@@ -477,10 +478,6 @@
             lg_forward(i).wait_send()
             part_send(i).wait_send()
 
-    query_out.wait()
-    for out in outs:
-        out.wait()
-
 
 def fused(q, k, v, lg, w, n_ctx, factor):
     tokens, width = lg.shape
@@ -488,7 +485,7 @@
     heads = columns // HEAD
     chunks = 8
     blocks = 4
-    pieces = 4
+    pieces = 2
     dma = pltpu.SemaphoreType.DMA
     vmem = pltpu.VMEM
     state = (heads, HEAD, HEAD)
@@ -498,25 +495,25 @@
     any_spec = pl.BlockSpec(memory_space=pl.ANY)
     return pl.pallas_call(
         functools.partial(gather_kernel, n_ctx, factor),
-        out_shape=[jax.ShapeDtypeStruct(whole, BF16)] * 3,
+        out_shape=[pltpu.VMEM(whole, BF16)] * 3,
         in_specs=[any_spec] * 5,
-        out_specs=[any_spec] * 3,
+        out_specs=[pl.BlockSpec(memory_space=pltpu.VMEM)] * 3,
         scratch_shapes=[
             vmem(whole, BF16), vmem(whole, BF16), vmem(whole, BF16), vmem(whole, BF16),
             vmem((tokens, 4 * width), BF16), vmem(w.shape, BF16), vmem((columns, 2 * width), BF16),
             vmem(whole, BF16), vmem(whole, BF16),
-            vmem(whole, BF16), vmem(whole, BF16), vmem(whole, BF16), vmem(whole, F32), vmem(whole, F32),
+            vmem(whole, F32), vmem(whole, F32),
             vmem((blocks,) + state, F32), vmem((blocks,) + state, BF16), vmem((blocks,) + state, F32), vmem(state, F32),
             vmem(state, BF16), vmem((n_ctx - 1,) + state, BF16), vmem(state, BF16), vmem(state, BF16),
             vmem(half, BF16), vmem((chips - 1,) + half, BF16), vmem(half, F32), vmem(half, F32),
             dma((5,)), dma((chunks,)), dma((chunks,)), dma((4, chunks)), dma((chunks,)),
             dma((chunks,)), dma((chunks,)),
-            dma((pieces,)), dma((pieces,)), dma((pieces,)), dma((pieces,)),
+            dma((pieces,)), dma((pieces,)), dma((3, pieces)), dma((3, pieces)),
             dma((n_ctx - 1,)), dma((n_ctx - 1,)), dma((chips - 1,)), dma((chips - 1,)),
-            dma((3,)), dma((3,)), dma((2 * blocks + 1,)),
+            dma((3,)), dma((3,)),
         ],
         compiler_params=pltpu.CompilerParams(
-            collective_id=0, has_side_effects=True, vmem_limit_bytes=62 * 1024 * 1024),
+            collective_id=0, has_side_effects=True, vmem_limit_bytes=54 * 1024 * 1024),
     )(q, k, v, lg, w)
 
 
@@ -542,7 +539,7 @@
     n_ctx = lax.axis_size("ctx")
     n_tp = lax.axis_size("tp")
     factor = float((HEAD * q.shape[0] * n_ctx) ** (-0.5))
-    if n_tp == 4 and n_ctx % 2 == 0 and n_ctx > 2 and q.shape[0] % 1024 == 0 and q.shape[1] % 256 == 0:
+    if n_tp == 4 and n_ctx % 4 == 0 and q.shape[0] % 1024 == 0 and q.shape[1] % 256 == 0:
         return tuple(fused(q, k, v, lg, w, n_ctx, factor))
     g, kv_before, grad_after = gather_plain(q, k, v, lg, w)
     return tuple(attention(q, k, v, g, kv_before, grad_after, factor))

time: 142 us -> 135 us (0.951)
  Pallas kernels: 134 us -> 130 us
  local copies, waits for them, and re-layouts: 6.9 us -> 3.96 us
    pallas_call x1, Pallas kernels: 134 us -> 130 us  [fused(): pl.pallas_call(functools.partial(gather_kernel, n_ctx, factor), out_shape...]
    unnamed x7 -> x3, local copies, waits for them, and re-layouts: 6.9 us -> 3.96 us
where the time goes in v4:
time: 135 us
  Pallas kernels  130 us (96%)
  local copies, waits for them, and re-layouts  3.96 us (3%)
    pallas_call x1, Pallas kernels, fused(): pl.pallas_call(functools.partial(gather_kernel, n_ctx, factor), out_shape...  130 us
    unnamed x3, local copies, waits for them, and re-layouts  3.96 us

profile of v4, /device:TPU:0, one launch (start us, length us, event | category | flops | bytes accessed | tf_op | source)
XLA Modules:
  0.0 134.6 jit_solution(3860584686614287161)
XLA Ops:
  0.6 130.0 %shard_map.76 = (bf16[1024,1024]{1,0:T(8,128)(2,1)S(1)}, bf16[1024,1024]{1,0:T(8,128)(2,1)S(1)}, bf16[1024,1024]{1,0:T(8,128)(2,1)S(1)}) custom-call(bf16[1024,1024]{1,0:T(8,128)(2,1)} %q_hbm.1, bf16[1024,1024]{1,0:T(8,128)(2,1)} %k_hbm.1, bf16[1024,1024]{1,0:T(8,128)(2,1)} %v_hbm.1, bf16[1024,1024]{1,0:T(8,128)(2,1)} %lg_hbm.1, bf16[1024,4096]{1,0:T(8,128)(2,1)} %w_hbm.1), custom_call_target="tpu_custom_call" | custom-call | tf_op jit(solution)/shard_map/pallas_call | solution.py:496
  130.6 1.3 copy.11
  132.0 1.3 copy.12
  133.3 1.3 copy.13

commit v5 on v4

--- a/solution.py
+++ b/solution.py
@@ -193,7 +193,7 @@
     blocks = kv_sums.shape[0]
     block = tokens // blocks
     per = chunks // blocks
-    ahead = 3
+    ahead = 3 * chunks // 8
     half_heads = heads // 2
     rows_at = lax.broadcasted_iota(jnp.int32, (block, block), 0)
     cols_at = lax.broadcasted_iota(jnp.int32, (block, block), 1)
@@ -218,7 +218,7 @@
     for load in loads[2:]:
         load.wait()
 
-    tile = min(256, columns)
+    tile = min(512, columns)
 
     def finish_kv():
         for d in range(1, n_ctx):
@@ -307,7 +307,7 @@
                 for p in range(pieces):
                     far_share(pal_share, p, 0, pal).wait_recv()
                     far_share(pal_share, p, 2, twin).start()
-            for i in {2: (0,), 3: (1, 2)}.get(c, ()):
+            for i in {2: range(ahead // 3), 3: range(ahead // 3, ahead)}.get(c, ()):
                 lg_arrival(end, i).wait_recv()
                 lg_forward(i).start()
             project(lg.at[:, middle], w.at[:, middle], key_part, span(c))
@@ -338,11 +338,15 @@
 
             part_send(i).start()
 
-            @pl.loop(0, columns // tile)
-            def _(n):
-                out = pl.ds(pl.multiple_of(n * tile, tile), tile)
-                total = key_part[row(i), out] + mm(lg[row(i), col(end)], w[out, col(end)], NT)
-                g_ref[row(i), out] = (total + mm(lg[row(i), col(end2)], w[out, col(end2)], NT)).astype(BF16)
+            @pl.when(i % 2 == 1)
+            def _():
+                both = pl.ds(pl.multiple_of((i // 2) * 2 * size, 2 * size), 2 * size)
+
+                @pl.loop(0, columns // tile)
+                def _(n):
+                    out = pl.ds(pl.multiple_of(n * tile, tile), tile)
+                    total = key_part[both, out] + mm(lg[both, col(end)], w[out, col(end)], NT)
+                    g_ref[both, out] = (total + mm(lg[both, col(end2)], w[out, col(end2)], NT)).astype(BF16)
 
             sum_step(i)
 

time: 135 us -> 132 us (0.978)
  Pallas kernels: 130 us -> 127 us
    pallas_call x1, Pallas kernels: 130 us -> 127 us  [fused(): pl.pallas_call(functools.partial(gather_kernel, n_ctx, factor), out_shape...]
where the time goes in v5:
time: 132 us; the launch traced here: 131 us
  Pallas kernels  127 us (96%)
  local copies, waits for them, and re-layouts  3.96 us (3%)
    pallas_call x1, Pallas kernels, fused(): pl.pallas_call(functools.partial(gather_kernel, n_ctx, factor), out_shape...  127 us
    unnamed x3, local copies, waits for them, and re-layouts  3.96 us

profile of v5, /device:TPU:0, one launch (start us, length us, event | category | flops | bytes accessed | tf_op | source)
XLA Modules:
  0.0 131.4 jit_solution(12568186389939667098)
XLA Ops:
  0.6 126.8 %shard_map.76 = (bf16[1024,1024]{1,0:T(8,128)(2,1)S(1)}, bf16[1024,1024]{1,0:T(8,128)(2,1)S(1)}, bf16[1024,1024]{1,0:T(8,128)(2,1)S(1)}) custom-call(bf16[1024,1024]{1,0:T(8,128)(2,1)} %q_hbm.1, bf16[1024,1024]{1,0:T(8,128)(2,1)} %k_hbm.1, bf16[1024,1024]{1,0:T(8,128)(2,1)} %v_hbm.1, bf16[1024,1024]{1,0:T(8,128)(2,1)} %lg_hbm.1, bf16[1024,4096]{1,0:T(8,128)(2,1)} %w_hbm.1), custom_call_target="tpu_custom_call" | custom-call | tf_op jit(solution)/shard_map/pallas_call | solution.py:500
  127.5 1.3 %copy.11 = bf16[1024,1024]{1,0:T(8,128)(2,1)} copy(bf16[1024,1024]{1,0:T(8,128)(2,1)S(1)} %get-tuple-element.3) | data formatting | bytes 4194304
  128.8 1.3 %copy.12 = bf16[1024,1024]{1,0:T(8,128)(2,1)} copy(bf16[1024,1024]{1,0:T(8,128)(2,1)S(1)} %get-tuple-element.4) | data formatting | bytes 4194304
  130.1 1.3 %copy.13 = bf16[1024,1024]{1,0:T(8,128)(2,1)} copy(bf16[1024,1024]{1,0:T(8,128)(2,1)S(1)} %get-tuple-element.5) | data formatting | bytes 4194304
